TPU v7x, 32 devices: a whole 2x2x4 slice. The times are simulated.
32 devices in a mesh: expert: 16 (over z, y, x), fsdp: 2 (over core).
Axes of the slice: x: 2, y: 2, z: 4, core: 2. Of those that a mesh axis runs over, the one named last changes fastest.
Arguments:
- tokens: bfloat16 [4096, 512], P(('expert', 'fsdp')), may hold values from -6 to 6
- out_grad: bfloat16 [4096, 512], P(('expert', 'fsdp')), may hold values from -6 to 6
- gates: bfloat16 [4096, 2], P('expert'), may hold values from 0.099609375 to 1
- expert_ids: int32 [4096, 2], P('expert'), may hold values from 0 to 15, as said below
- w_in: bfloat16 [16, 512, 4096], P('expert', None, 'fsdp'), may hold values from -0.25 to 0.25
- w_out: bfloat16 [16, 512, 4096], P('expert', None, 'fsdp'), may hold values from -0.09375 to 0.09375
Outputs:
- d_tokens: bfloat16 [4096, 512], P(('expert', 'fsdp'))
- d_gates: float32 [4096, 2], P(('expert', 'fsdp'))
- d_w_in: bfloat16 [16, 512, 4096], P('expert', None, 'fsdp')
- d_w_out: bfloat16 [16, 512, 4096], P('expert', None, 'fsdp')
Inputs may be any that keep to these rules, and one draw needn't show every extreme that they name: `expert_ids`: each token names two different experts. Within each aligned block of 128 tokens (the tokens of one device) no expert is named more than 20 times, and in every block some expert is named exactly 20 times.
All inputs are finite; a program needn't handle non-finite values.
Results may differ from a plain program's by a relative error of at most 0.011.
Values may be sent and summed in bfloat16 or wider, within the bound.
No kernel may reach another device: no remote copies, remote signals or barrier semaphores. Data moves between devices by JAX's collectives and lax.ppermute only.
A program may use at most 64 MiB of HBM per device.

v0:
```python
import functools

import jax
import jax.numpy as jnp
from jax import lax
from jax.experimental import pallas as pl
from jax.experimental.pallas import tpu as pltpu
from jax.sharding import PartitionSpec as P


COEF = 0.7978845608
CUBIC = 0.044715
ROW_DIMS = (((0,), (0,)), ((), ()))
LAST_DIMS = (((1,), (1,)), ((), ()))
LANES = 128
TILE = 8
PACK = 16
MIB = 1 << 20


def gelu_parts(pre_act):
    square = pre_act * pre_act
    half = 0.5 + 0.5 * jnp.tanh(pre_act * (COEF + (COEF * CUBIC) * square))
    values = pre_act * half
    slopes = half + values * ((1.0 - half) * (2.0 * COEF + (6.0 * COEF * CUBIC) * square))
    return values, slopes


def iota(shape, dim):
    return lax.broadcasted_iota(jnp.int32, shape, dim)


def one_hot(mask):
    return jnp.where(mask, 1.0, 0.0).astype(jnp.bfloat16)


class Plan:
    def __init__(self, experts, groups, tok_dev, width):
        self.experts, self.groups, self.tok_dev, self.width = experts, groups, tok_dev, width
        self.cap = 5 * tok_dev // (2 * experts)
        self.main = self.cap // PACK * PACK
        self.tail = self.cap - self.main
        self.send = 2 * self.cap
        self.back = self.main + TILE
        self.slots = experts * self.cap
        self.heads = experts * self.main

    def fits(self):
        return (
            self.groups == 2
            and self.main > 0
            and 2 * self.tail == TILE
            and self.cap <= LANES
            and self.tok_dev % LANES == 0
            and self.width % LANES == 0
        )


def dispatch_kernel(plan, ids_ref, gates_ref, x_ref, dy_ref, send_ref, route_ref):
    tokens = plan.tok_dev
    mine = pl.ds(pl.multiple_of(lax.axis_index("fsdp") * tokens, LANES), tokens)
    ids = ids_ref[:, mine]
    gates = gates_ref[:, mine].astype(jnp.float32)
    expert = iota((plan.experts, tokens), 0)
    named = [expert == ids[k : k + 1, :] for k in range(2)]
    earlier = one_hot(iota((tokens, tokens), 0) < iota((tokens, tokens), 1))
    counts = jnp.dot(one_hot(named[0] | named[1]), earlier, preferred_element_type=jnp.float32)
    row = iota((plan.experts * plan.send, tokens), 0)
    x_pick, dy_pick = False, 0.0
    for k in range(2):
        rank = jnp.sum(jnp.where(named[k], counts, 0.0), axis=0, keepdims=True).astype(jnp.int32)
        first = ids[k : k + 1, :] * plan.send + rank
        head = rank < plan.main
        x_pick = x_pick | (row == first + jnp.where(head, 0, plan.main))
        dy_pick = dy_pick + jnp.where(
            row == first + jnp.where(head, plan.main, plan.cap), gates[k : k + 1, :], 0.0
        )
        route_ref[k : k + 1, :] = ids[k : k + 1, :]
        route_ref[2 + k : 3 + k, :] = rank
        route_ref[4 + k : 5 + k, :] = jnp.zeros_like(rank)
        route_ref[6 + k : 7 + k, :] = jnp.zeros_like(rank)
    send = jnp.dot(one_hot(x_pick), x_ref[...], preferred_element_type=jnp.float32)
    send = send + jnp.dot(
        dy_pick.astype(jnp.bfloat16), dy_ref[...], preferred_element_type=jnp.float32
    )
    send_ref[...] = send.astype(jnp.bfloat16)


def unpack(plan, recv_ref, x_all, dy_all, at):
    main, tail, width = plan.main, plan.tail, plan.width
    tails = plan.experts * tail
    heads = pl.ds(at, plan.heads)
    x_all[heads, :] = recv_ref[:, :main, :].reshape(plan.heads, width)
    dy_all[heads, :] = recv_ref[:, main : 2 * main, :].reshape(plan.heads, width)
    mixed = recv_ref[:, 2 * main :, :].reshape(plan.experts * TILE, width)
    place, source = iota((2 * tails, plan.experts * TILE), 0), iota(
        (2 * tails, plan.experts * TILE), 1
    )
    second = jnp.where(place >= tails, 1, 0)
    slot = place - second * tails
    pick = one_hot(source == slot // tail * TILE + slot % tail + second * tail)
    split = jnp.dot(pick, mixed, preferred_element_type=jnp.float32).astype(jnp.bfloat16)
    x_all[pl.ds(at + plan.heads, tails), :] = split[:tails]
    dy_all[pl.ds(at + plan.heads, tails), :] = split[tails:]


def column_copies(sources, buffers, sems):
    block = buffers[0].shape[2]
    copies = []
    for pair in sources:
        for at in range(0, pair[0].shape[1], block):
            n = len(copies)
            copies.append(
                [
                    pltpu.make_async_copy(
                        ref.at[:, at : at + block], buffers[m].at[n], sems.at[m, n]
                    )
                    for m, ref in enumerate(pair)
                ]
            )
    return copies


def staged(count, ahead, finish):
    held = ahead(0)
    for n in range(count):
        later = ahead(n + 1) if n + 1 < count else None
        finish(n, *held)
        held = later


def first_acts(x_all, dy_all, buffers, copies, part):
    block = buffers[0].shape[2]

    def ahead(n):
        chunk, at = divmod(n * part, block)
        if at == 0:
            for copy in copies[chunk]:
                copy.wait()
        return tuple(
            jnp.dot(
                rows[...], mat[chunk, :, at : at + part], preferred_element_type=jnp.float32
            )
            for rows, mat in zip((x_all, dy_all), buffers)
        )

    return ahead


def token_kernel(
    plan, part, recv_ref, in_a, out_a, in_b, out_b, back_ref, x_all, dy_all, total, in_buf, out_buf, sems
):
    buffers = (in_buf, out_buf)
    copies = column_copies(((in_a, out_a), (in_b, out_b)), buffers, sems)
    for pair in copies:
        for copy in pair:
            copy.start()
    unpack(plan, recv_ref, x_all, dy_all, 0)
    block = in_buf.shape[2]
    gate_lanes = []

    def finish(n, pre_act, grad_act):
        chunk, at = divmod(n * part, block)
        values, slopes = gelu_parts(pre_act)
        grad_pre = (grad_act * slopes).astype(jnp.bfloat16)
        back = lax.dot_general(
            grad_pre,
            in_buf[chunk, :, at : at + part],
            LAST_DIMS,
            preferred_element_type=jnp.float32,
        )
        total[...] = back if n == 0 else total[...] + back
        product = grad_act * values
        for lane in range(0, part, LANES):
            piece = product[:, lane : lane + LANES]
            gate_lanes[:] = [gate_lanes[0] + piece] if gate_lanes else [piece]

    staged(len(copies) * block // part, first_acts(x_all, dy_all, buffers, copies, part), finish)

    main, tail, width = plan.main, plan.tail, plan.width
    tails = plan.experts * tail
    rows = total[...].astype(jnp.bfloat16)
    back_ref[:, :main, :] = rows[: plan.heads].reshape(plan.experts, main, width)
    gate = jnp.sum(gate_lanes[0], axis=1, keepdims=True)
    slot = iota((plan.slots, LANES), 0)
    over = slot - plan.heads
    rank = jnp.where(over >= 0, main + over % tail, slot % main)
    gate_rows = jnp.where(iota((plan.slots, LANES), 1) == rank, gate, 0.0).astype(jnp.bfloat16)
    place, slot = iota((plan.experts * TILE, plan.slots), 0), iota(
        (plan.experts * TILE, plan.slots), 1
    )
    over = slot - plan.heads
    source = jnp.where(over >= 0, over // tail, slot // main)
    gates = jnp.dot(
        one_hot(place == source * TILE + tail), gate_rows, preferred_element_type=jnp.float32
    )
    place, slot = iota((plan.experts * TILE, tails), 0), iota((plan.experts * TILE, tails), 1)
    rest = jnp.dot(
        one_hot(place == slot // tail * TILE + slot % tail),
        rows[plan.heads :],
        preferred_element_type=jnp.float32,
    )
    rest = jnp.concatenate([rest[:, :LANES] + gates, rest[:, LANES:]], axis=1)
    back_ref[:, main:, :] = rest.astype(jnp.bfloat16).reshape(plan.experts, TILE, width)


def weight_kernel(
    plan,
    part,
    own_ref,
    other_ref,
    in_ref,
    out_ref,
    grad_in_ref,
    grad_out_ref,
    x_all,
    dy_all,
    x_turned,
    dy_turned,
    in_buf,
    out_buf,
    in_grads,
    out_grads,
    sems,
    done,
):
    buffers = (in_buf, out_buf)
    copies = column_copies(((in_ref, out_ref),), buffers, sems)
    for pair in copies:
        for copy in pair:
            copy.start()
    unpack(plan, own_ref, x_all, dy_all, 0)
    unpack(plan, other_ref, x_all, dy_all, plan.slots)
    x_turned[...] = x_all[...].T
    dy_turned[...] = dy_all[...].T
    block = in_buf.shape[2]
    stores = []

    def finish(n, pre_act, grad_act):
        chunk, at = divmod(n * part, block)
        values, slopes = gelu_parts(pre_act)
        grad_pre = (grad_act * slopes).astype(jnp.bfloat16)
        for rows, acts, held in (
            (x_turned, grad_pre, in_grads),
            (dy_turned, values.astype(jnp.bfloat16), out_grads),
        ):
            held[chunk, :, at : at + part] = jnp.dot(
                rows[...], acts, preferred_element_type=jnp.float32
            ).astype(jnp.bfloat16)
        if at + part == block:
            columns = slice(chunk * block, (chunk + 1) * block)
            for m, (held, ref) in enumerate(((in_grads, grad_in_ref), (out_grads, grad_out_ref))):
                stores.append(
                    pltpu.make_async_copy(held.at[chunk], ref.at[:, columns], done.at[m, chunk])
                )
                stores[-1].start()

    staged(len(copies) * block // part, first_acts(x_all, dy_all, buffers, copies, part), finish)
    for store in stores:
        store.wait()


def place_kernel(plan, route_ref, pick_ref):
    row = iota((plan.experts * plan.back, plan.tok_dev), 0)
    pick = False
    for k in range(2):
        pick = pick | (row == route_ref[k : k + 1, :] * plan.back + route_ref[2 + k : 3 + k, :])
    pick_ref[...] = jnp.where(pick, 1.0, 0.0).T.astype(jnp.bfloat16)


def combine_kernel(plan, route_ref, pick_ref, gates_ref, back_ref, token_ref, gate_ref):
    tokens, rows = plan.tok_dev, plan.experts * plan.back
    mine = pl.ds(pl.multiple_of(lax.axis_index("fsdp") * tokens, LANES), tokens)
    gates = gates_ref[:, mine].astype(jnp.float32)
    back = back_ref[...]
    token_ref[...] = jnp.dot(
        pick_ref[...], back, preferred_element_type=jnp.float32
    ).astype(jnp.bfloat16)
    gate_row = iota((plan.experts, rows), 0) * plan.back + plan.cap
    gate_rows = jnp.dot(
        one_hot(iota((plan.experts, rows), 1) == gate_row),
        back[:, :LANES],
        preferred_element_type=jnp.float32,
    ).astype(jnp.bfloat16)
    for k in range(2):
        named = one_hot(iota((plan.experts, tokens), 0) == route_ref[k : k + 1, :])
        slots = lax.dot_general(gate_rows, named, ROW_DIMS, preferred_element_type=jnp.float32)
        here = iota((LANES, tokens), 0) == route_ref[2 + k : 3 + k, :]
        total = jnp.sum(jnp.where(here, slots, 0.0), axis=0, keepdims=True)
        gate_ref[k : k + 1, :] = total / gates[k : k + 1, :]


def params(mib):
    return pltpu.CompilerParams(vmem_limit_bytes=mib * MIB)


def moved_rows(plan, tokens, out_grad, gates, expert_ids, w_in, w_out):
    experts, width, slots = plan.experts, plan.width, plan.slots
    in_own, out_own = w_in[0], w_out[0]
    hidden = in_own.shape[1]
    swap = [(0, 1), (1, 0)]
    in_other = lax.ppermute(in_own, "fsdp", swap)
    out_other = lax.ppermute(out_own, "fsdp", swap)
    ids, gate_rows = expert_ids.T, gates.T
    bf16, f32 = jnp.bfloat16, jnp.float32

    send, route = pl.pallas_call(
        functools.partial(dispatch_kernel, plan),
        out_shape=(
            jax.ShapeDtypeStruct((experts * plan.send, width), bf16),
            jax.ShapeDtypeStruct((TILE, plan.tok_dev), jnp.int32),
        ),
        name="dispatch",
    )(ids, gate_rows, tokens, out_grad)
    recv = lax.all_to_all(
        send.reshape(experts, plan.send, width),
        "expert",
        split_axis=0,
        concat_axis=0,
        tiled=True,
    )
    recv_other = lax.ppermute(recv, "fsdp", swap)
    pick = pl.pallas_call(
        functools.partial(place_kernel, plan),
        out_shape=jax.ShapeDtypeStruct((plan.tok_dev, experts * plan.back), bf16),
        compiler_params=params(63),
        name="placing",
    )(route)

    block, part = min(256, hidden), min(256, hidden)
    blocks = hidden // block
    anywhere, held = pl.BlockSpec(memory_space=pl.ANY), pl.BlockSpec(memory_space=pltpu.VMEM)
    dma = pltpu.SemaphoreType.DMA

    def matrix(*shape):
        return pltpu.VMEM(shape, bf16)

    back = pl.pallas_call(
        functools.partial(token_kernel, plan, part),
        in_specs=[held] + [anywhere] * 4,
        out_specs=held,
        out_shape=jax.ShapeDtypeStruct((experts, plan.back, width), bf16),
        scratch_shapes=[
            matrix(slots, width),
            matrix(slots, width),
            pltpu.VMEM((slots, width), f32),
            matrix(2 * blocks, width, block),
            matrix(2 * blocks, width, block),
            dma((2, 2 * blocks)),
        ],
        cost_estimate=pl.CostEstimate(
            flops=12 * slots * width * hidden,
            transcendentals=2 * slots * hidden,
            bytes_accessed=8 * width * hidden,
        ),
        compiler_params=params(52),
        name="token_grad",
    )(recv, in_own, out_own, in_other, out_other)
    returned = lax.all_to_all(back, "expert", split_axis=0, concat_axis=0, tiled=True)

    grad_in, grad_out = pl.pallas_call(
        functools.partial(weight_kernel, plan, part),
        in_specs=[held, held, anywhere, anywhere],
        out_specs=(anywhere, anywhere),
        out_shape=(jax.ShapeDtypeStruct((width, hidden), bf16),) * 2,
        scratch_shapes=[
            matrix(2 * slots, width),
            matrix(2 * slots, width),
            matrix(width, 2 * slots),
            matrix(width, 2 * slots),
            matrix(blocks, width, block),
            matrix(blocks, width, block),
            matrix(blocks, width, block),
            matrix(blocks, width, block),
            dma((2, blocks)),
            dma((2, blocks)),
        ],
        cost_estimate=pl.CostEstimate(
            flops=16 * slots * width * hidden,
            transcendentals=2 * slots * hidden,
            bytes_accessed=8 * width * hidden,
        ),
        compiler_params=params(52),
        name="weight_grad",
    )(recv, recv_other, in_own, out_own)

    d_tokens, d_gates = pl.pallas_call(
        functools.partial(combine_kernel, plan),
        out_shape=(
            jax.ShapeDtypeStruct((plan.tok_dev, width), bf16),
            jax.ShapeDtypeStruct((2, plan.tok_dev), f32),
        ),
        compiler_params=params(16),
        name="combine",
    )(route, pick, gate_rows, returned.reshape(experts * plan.back, width))
    return d_tokens, d_gates.T, grad_in[None], grad_out[None]


def slot_ranks(route_ids):
    count = route_ids.shape[1]
    same = route_ids[:, :, None] == route_ids[:, None, :]
    earlier = jnp.arange(count)[None, :] < jnp.arange(count)[:, None]
    return jnp.sum(jnp.logical_and(same, earlier[None]), axis=2)


def fill_slots(owner, rows_x, rows_dy, gate_flat):
    valid = owner >= 0
    safe = jnp.where(valid, owner, 0)
    token_row = safe // 2
    x_buf = jnp.where(valid[:, None], rows_x[token_row], jnp.zeros((), rows_x.dtype))
    dy_buf = jnp.where(valid[:, None], rows_dy[token_row], jnp.zeros((), rows_dy.dtype))
    gate_buf = jnp.where(valid, gate_flat[safe], jnp.zeros((), gate_flat.dtype))
    return (x_buf, dy_buf, gate_buf)


def expert_work(x_rows, dy_rows, gate_rows, in_shard, out_shard):
    pre_act = jnp.dot(x_rows, in_shard, preferred_element_type=jnp.float32)
    grad_act = jnp.dot(dy_rows, out_shard, preferred_element_type=jnp.float32)
    values, slopes = gelu_parts(pre_act)
    scale = gate_rows.astype(jnp.float32)[:, None]
    act_scaled = (scale * values).astype(jnp.bfloat16)
    grad_pre = (scale * grad_act * slopes).astype(jnp.bfloat16)
    grad_out = lax.dot_general(dy_rows, act_scaled, ROW_DIMS, preferred_element_type=jnp.float32)
    grad_in = lax.dot_general(x_rows, grad_pre, ROW_DIMS, preferred_element_type=jnp.float32)
    token_part = lax.dot_general(
        grad_pre, in_shard, LAST_DIMS, preferred_element_type=jnp.float32
    ).astype(jnp.bfloat16)
    gate_part = jnp.sum(grad_act * values, axis=1).astype(jnp.bfloat16)
    return (grad_in, grad_out, token_part, gate_part)


def all_rows(plan, tokens, out_grad, gates, expert_ids, w_in, w_out):
    tok_dev, width, groups = plan.tok_dev, plan.width, plan.groups
    experts, capacity = plan.experts, plan.cap
    group_ids = expert_ids.reshape(groups, 2 * tok_dev)
    group_gates = gates.reshape(groups, 2 * tok_dev)
    group_ranks = slot_ranks(group_ids)
    all_x = lax.all_gather(tokens, "fsdp", axis=0, tiled=True)
    all_dy = lax.all_gather(out_grad, "fsdp", axis=0, tiled=True)
    member = jnp.arange(groups, dtype=jnp.int32)[:, None]
    target = ((group_ids * groups + member) * capacity + group_ranks).reshape(-1)
    owner = (
        jnp.full((experts * groups * capacity,), -1, jnp.int32)
        .at[target]
        .set(jnp.arange(2 * tok_dev * groups, dtype=jnp.int32))
    )
    span = groups * capacity
    total_rows = experts * span

    def exchange(rows):
        rows = rows.reshape((experts, span) + rows.shape[1:])
        rows = lax.all_to_all(rows, "expert", split_axis=0, concat_axis=0, tiled=True)
        return rows.reshape((total_rows,) + rows.shape[2:])

    buffers = fill_slots(owner, all_x, all_dy, group_gates.reshape(-1))
    grad_in, grad_out, token_part, gate_part = expert_work(
        *(exchange(b) for b in buffers), w_in[0], w_out[0]
    )
    token_back, gate_back = exchange(token_part), exchange(gate_part)
    token_pick = token_back[target].astype(jnp.float32).reshape(groups * tok_dev, 2, width)
    gate_terms = gate_back[target].astype(jnp.float32).reshape(groups * tok_dev, 2)

    def spread(terms):
        return lax.psum_scatter(
            terms.astype(jnp.bfloat16), "fsdp", scatter_dimension=0, tiled=True
        )

    return (
        spread(jnp.sum(token_pick, axis=1)).astype(jnp.bfloat16),
        spread(gate_terms).astype(jnp.float32),
        grad_in.astype(jnp.bfloat16)[None],
        grad_out.astype(jnp.bfloat16)[None],
    )


def per_device(tokens, out_grad, gates, expert_ids, w_in, w_out):
    plan = Plan(lax.axis_size("expert"), lax.axis_size("fsdp"), *tokens.shape)
    form = moved_rows if plan.fits() else all_rows
    return form(plan, tokens, out_grad, gates, expert_ids, w_in, w_out)


def solution(mesh):
    rows, both = P(("expert", "fsdp"), None), P("expert", None)
    weights = P("expert", None, "fsdp")
    return jax.shard_map(
        per_device,
        mesh=mesh,
        in_specs=(rows, rows, both, both, weights, weights),
        out_specs=(rows, rows, weights, weights),
        check_vma=False,
    )
```

profile of v0, /device:TPU:0, one launch (start us, length us, event | category | flops | bytes accessed | tf_op | source)
XLA Modules:
  0.0 59.8 jit_solution(2718157987577294298)
XLA Ops:
  0.6 0.6 collective-permute-start
  1.2 0.1 collective-permute-start.1
  1.3 2.5 %dispatch.1 = (bf16[640,512]{1,0:T(8,128)(2,1)}, s32[8,128]{1,0:T(8,128)}) custom-call(s32[2,256]{1,0:T(2,128)} %bitcast.13, bf16[2,256]{1,0:T(2,128)(2,1)} %bitcast.10, bf16[128,512]{1,0:T(8,128)(2,1)} %x_ref.1, bf16[128,512]{1,0:T(8,128)(2,1)} %dy_ref.1), custom_call_target="tpu_custom_call" | custom-call | tf_op jit(solution)/shard_map/dispatch/pallas_call | solution.py:307
  3.8 27.4 %all_to_all.10.recv_ref.own_ref = bf16[16,40,512]{2,1,0:T(8,128)(2,1)} all-to-all(bf16[16,40,512]{2,1,0:T(8,128)(2,1)} %bitcast.12), channel_id=1, replica_groups=mesh['expert'=16,'fsdp'=2] {'expert'}, dimensions={0} | all-to-all | bytes 1310720 | tf_op jit(solution)/shard_map/all_to_all | solution.py:315
  31.2 0.0 collective-permute-start.2
  31.2 0.0 collective-permute-done.in_b
  31.2 0.0 copy-start.3
  31.2 0.0 collective-permute-done.1.out_b
  31.2 1.3 %copy-done.3 = bf16[512,2048]{1,0:T(8,128)(2,1)} copy-done((bf16[512,2048]{1,0:T(8,128)(2,1)}, bf16[512,2048]{1,0:T(8,128)(2,1)S(1)}, u32[]{:S(2)}) %copy-start.3) | copy-done | bytes 2097176
  32.5 9.5 %token_grad.1 = bf16[16,24,512]{2,1,0:T(8,128)(2,1)} custom-call(bf16[16,40,512]{2,1,0:T(8,128)(2,1)} %all_to_all.10.recv_ref.own_ref, bf16[512,2048]{1,0:T(8,128)(2,1)} %bitcast.15, bf16[512,2048]{1,0:T(8,128)(2,1)} %bitcast.18, bf16[512,2048]{1,0:T(8,128)(2,1)} %copy-done.3, bf16[512,2048]{1,0:T(8,128)(2,1)} %collective-permute-done.1.out_b), custom_call_target="tpu_custom_call" | custom-call | flops 4026531840 | bytes 8388608 | tf_op jit(solution)/shard_map/token_grad/pallas_call | solution.py:338
  42.0 3.7 %all-to-all-start.1 = ((bf16[16,24,512]{2,1,0:T(8,128)(2,1)}), bf16[16,24,512]{2,1,0:T(8,128)(2,1)S(1)}, u32[]{:S(2)}, u32[]{:S(2)}) async-start(bf16[16,24,512]{2,1,0:T(8,128)(2,1)} %token_grad.1), calls=%async_computation.1 | async-start | bytes 786432 | tf_op jit(solution)/shard_map/all_to_all | solution.py:359
  45.8 1.4 %placing.1.pick_ref = bf16[128,384]{1,0:T(8,128)(2,1)} custom-call(s32[8,128]{1,0:T(8,128)} %get-tuple-element.10.route_ref), custom_call_target="tpu_custom_call" | custom-call | tf_op jit(solution)/shard_map/placing/pallas_call | solution.py:323
  47.2 0.0 copy-start
  47.2 0.0 copy-start.1
  47.2 0.0 copy-start.2
  47.2 0.0 collective-permute-done.2.other_ref
  47.2 11.0 %weight_grad.1 = (bf16[512,2048]{1,0:T(8,128)(2,1)}, bf16[512,2048]{1,0:T(8,128)(2,1)}) custom-call(bf16[16,40,512]{2,1,0:T(8,128)(2,1)} %all_to_all.10.recv_ref.own_ref, bf16[16,40,512]{2,1,0:T(8,128)(2,1)} %collective-permute-done.2.other_ref, bf16[512,2048]{1,0:T(8,128)(2,1)} %bitcast.16, bf16[512,2048]{1,0:T(8,128)(2,1)} %bitcast.19), custom_call_target="tpu_custom_call" | custom-call | flops 5368709120 | bytes 8388608 | tf_op jit(solution)/shard_map/weight_grad/pallas_call | solution.py:361
  58.2 0.5 all-to-all-done.1
  58.7 0.0 copy-done
  58.7 0.0 copy-done.1
  58.7 0.0 copy-done.2
  58.7 1.0 %combine.1 = (bf16[128,512]{1,0:T(8,128)(2,1)}, f32[2,128]{1,0:T(2,128)}) custom-call(s32[8,128]{1,0:T(8,128)S(1)} %copy-done.1, bf16[128,384]{1,0:T(8,128)(2,1)S(1)} %copy-done, bf16[2,256]{1,0:T(2,128)(2,1)S(1)} %bitcast.11, bf16[384,512]{1,0:T(8,128)(2,1)S(1)} %bitcast.9), custom_call_target="tpu_custom_call" | custom-call | tf_op jit(solution)/shard_map/combine/pallas_call | solution.py:387
Async XLA Ops:
  0.6 30.5 %collective-permute-start = (bf16[512,2048]{1,0:T(8,128)(2,1)}, bf16[512,2048]{1,0:T(8,128)(2,1)S(1)}, u32[]{:S(2)}, u32[]{:S(2)}) collective-permute-start(bf16[512,2048]{1,0:T(8,128)(2,1)} %bitcast.14), channel_id=1, source_target_pairs={{0,1},{1,0},{2,3},{3,2},{4,5},{5,4},{6,7},{7,6},{8,9},{9,8},{10,11... | collective-permute-start | bytes 6291464 | tf_op jit(solution)/shard_map/ppermute | solution.py:302
  1.2 30.0 %collective-permute-start.1 = (bf16[512,2048]{1,0:T(8,128)(2,1)}, bf16[512,2048]{1,0:T(8,128)(2,1)}, u32[]{:S(2)}, u32[]{:S(2)}) collective-permute-start(bf16[512,2048]{1,0:T(8,128)(2,1)} %bitcast.17), channel_id=1, source_target_pairs={{0,1},{1,0},{2,3},{3,2},{4,5},{5,4},{6,7},{7,6},{8,9},{9,8},{10,11... | collective-permute-start | bytes 6291464 | tf_op jit(solution)/shard_map/ppermute | solution.py:303
  31.2 16.0 %collective-permute-start.2 = (bf16[16,40,512]{2,1,0:T(8,128)(2,1)}, bf16[16,40,512]{2,1,0:T(8,128)(2,1)}, u32[]{:S(2)}, u32[]{:S(2)}) collective-permute-start(bf16[16,40,512]{2,1,0:T(8,128)(2,1)} %all_to_all.10.recv_ref.own_ref), channel_id=1, source_target_pairs={{0,1},{1,0},{2,3},{3,2},{4,5},{5,4},{6,7},{7,6},{8,9},{9,8},{10,11... | collective-permute-start | bytes 1966088 | tf_op jit(solution)/shard_map/ppermute | solution.py:322
  31.2 1.3 %copy-start.3 = (bf16[512,2048]{1,0:T(8,128)(2,1)}, bf16[512,2048]{1,0:T(8,128)(2,1)S(1)}, u32[]{:S(2)}) copy-start(bf16[512,2048]{1,0:T(8,128)(2,1)S(1)} %collective-permute-done.in_b) | copy-start | bytes 6291460
  42.0 16.7 %all-to-all-start.1 = ((bf16[16,24,512]{2,1,0:T(8,128)(2,1)}), bf16[16,24,512]{2,1,0:T(8,128)(2,1)S(1)}, u32[]{:S(2)}, u32[]{:S(2)}) async-start(bf16[16,24,512]{2,1,0:T(8,128)(2,1)} %token_grad.1), calls=%async_computation.1 | async-start | bytes 786432 | tf_op jit(solution)/shard_map/all_to_all | solution.py:359
  47.2 11.6 %copy-start = (bf16[128,384]{1,0:T(8,128)(2,1)S(1)}, bf16[128,384]{1,0:T(8,128)(2,1)}, u32[]{:S(2)}) copy-start(bf16[128,384]{1,0:T(8,128)(2,1)} %placing.1.pick_ref) | copy-start | bytes 294916
  47.2 11.6 %copy-start.1 = (s32[8,128]{1,0:T(8,128)S(1)}, s32[8,128]{1,0:T(8,128)}, u32[]{:S(2)}) copy-start(s32[8,128]{1,0:T(8,128)} %get-tuple-element.10.route_ref) | copy-start | bytes 12292
  47.2 11.6 %copy-start.2 = (bf16[256,2]{0,1:T(2,128)(2,1)S(1)}, bf16[256,2]{0,1:T(2,128)(2,1)}, u32[]{:S(2)}) copy-start(bf16[256,2]{0,1:T(2,128)(2,1)} %param.8) | copy-start | bytes 3076
where the time goes:
time: 60.2 us; the launch traced here: 59.8 us
  blocking collectives  27.4 us (46%)
  Pallas kernels  25.5 us (42%)
  starting transfers between devices  4.39 us (7%)
  local copies, waits for them, and re-layouts  1.32 us (2%)
  between operations  0.68 us (1%)
    all_to_all x1, blocking collectives, moved_rows(): lax.all_to_all(send.reshape(experts, plan.send, width), 'expert', split_a...  27.4 us
    pallas_call x1, Pallas kernels, moved_rows(): pl.pallas_call(functools.partial(weight_kernel, plan, part), in_specs=[he...  11 us
    pallas_call x1, Pallas kernels, moved_rows(): pl.pallas_call(functools.partial(token_kernel, plan, part), in_specs=[hel...  9.51 us
    all_to_all x1, starting transfers between devices, moved_rows(): lax.all_to_all(back, 'expert', split_axis=0, concat_axis=0, tiled=True)  3.74 us
    pallas_call x1, Pallas kernels, moved_rows(): pl.pallas_call(functools.partial(dispatch_kernel, plan), out_shape=(jax.S...  2.49 us
    pallas_call x1, Pallas kernels, moved_rows(): pl.pallas_call(functools.partial(place_kernel, plan), out_shape=jax.Shape...  1.42 us
    unnamed x8, local copies, waits for them, and re-layouts  1.32 us
  transfers between devices with their start and end apart: 4, of which 1 were waited for; matrix products, arithmetic and copies ran while one was open for 0% of the time, Pallas kernels for 41%

commit v1 on v0

--- a/solution.py
+++ b/solution.py
@@ -48,7 +48,7 @@
     def fits(self):
         return (
             self.groups == 2
-            and self.main > 0
+            and self.main == PACK
             and 2 * self.tail == TILE
             and self.cap <= LANES
             and self.tok_dev % LANES == 0
@@ -104,6 +104,18 @@
     dy_all[pl.ds(at + plan.heads, tails), :] = split[tails:]
 
 
+def stage_kernel(_, in_hbm, out_hbm, in_first, out_first, sems):
+    columns = slice(0, in_first.shape[1])
+    copies = [
+        pltpu.make_async_copy(ref.at[:, columns], first, sems.at[m])
+        for m, (ref, first) in enumerate(((in_hbm, in_first), (out_hbm, out_first)))
+    ]
+    for copy in copies:
+        copy.start()
+    for copy in copies:
+        copy.wait()
+
+
 def column_copies(sources, buffers, sems):
     block = buffers[0].shape[2]
     copies = []
@@ -129,30 +141,35 @@
         held = later
 
 
-def first_acts(x_all, dy_all, buffers, copies, part):
+def part_of(first, buffer, n, part):
+    chunk, at = divmod(n * part, buffer.shape[2])
+    return first[:, at : at + part] if chunk == 0 else buffer[chunk, :, at : at + part]
+
+
+def first_acts(x_all, dy_all, firsts, buffers, copies, part):
     block = buffers[0].shape[2]
 
     def ahead(n):
         chunk, at = divmod(n * part, block)
-        if at == 0:
+        if at == 0 and chunk > 0:
             for copy in copies[chunk]:
                 copy.wait()
         return tuple(
             jnp.dot(
-                rows[...], mat[chunk, :, at : at + part], preferred_element_type=jnp.float32
+                rows[...], part_of(first, mat, n, part), preferred_element_type=jnp.float32
             )
-            for rows, mat in zip((x_all, dy_all), buffers)
+            for rows, first, mat in zip((x_all, dy_all), firsts, buffers)
         )
 
     return ahead
 
 
 def token_kernel(
-    plan, part, recv_ref, in_a, out_a, in_b, out_b, back_ref, x_all, dy_all, total, in_buf, out_buf, sems
+    plan, part, recv_ref, in_first, out_first, in_a, out_a, in_b, out_b, back_ref, x_all, dy_all, total, in_buf, out_buf, sems
 ):
-    buffers = (in_buf, out_buf)
+    buffers, firsts = (in_buf, out_buf), (in_first, out_first)
     copies = column_copies(((in_a, out_a), (in_b, out_b)), buffers, sems)
-    for pair in copies:
+    for pair in copies[1:]:
         for copy in pair:
             copy.start()
     unpack(plan, recv_ref, x_all, dy_all, 0)
@@ -160,12 +177,11 @@
     gate_lanes = []
 
     def finish(n, pre_act, grad_act):
-        chunk, at = divmod(n * part, block)
         values, slopes = gelu_parts(pre_act)
         grad_pre = (grad_act * slopes).astype(jnp.bfloat16)
         back = lax.dot_general(
             grad_pre,
-            in_buf[chunk, :, at : at + part],
+            part_of(in_first, in_buf, n, part),
             LAST_DIMS,
             preferred_element_type=jnp.float32,
         )
@@ -175,7 +191,7 @@
             piece = product[:, lane : lane + LANES]
             gate_lanes[:] = [gate_lanes[0] + piece] if gate_lanes else [piece]
 
-    staged(len(copies) * block // part, first_acts(x_all, dy_all, buffers, copies, part), finish)
+    staged(len(copies) * block // part, first_acts(x_all, dy_all, firsts, buffers, copies, part), finish)
 
     main, tail, width = plan.main, plan.tail, plan.width
     tails = plan.experts * tail
@@ -209,6 +225,8 @@
     part,
     own_ref,
     other_ref,
+    in_first,
+    out_first,
     in_ref,
     out_ref,
     grad_in_ref,
@@ -224,9 +242,9 @@
     sems,
     done,
 ):
-    buffers = (in_buf, out_buf)
+    buffers, firsts = (in_buf, out_buf), (in_first, out_first)
     copies = column_copies(((in_ref, out_ref),), buffers, sems)
-    for pair in copies:
+    for pair in copies[1:]:
         for copy in pair:
             copy.start()
     unpack(plan, own_ref, x_all, dy_all, 0)
@@ -255,7 +273,7 @@
                 )
                 stores[-1].start()
 
-    staged(len(copies) * block // part, first_acts(x_all, dy_all, buffers, copies, part), finish)
+    staged(len(copies) * block // part, first_acts(x_all, dy_all, firsts, buffers, copies, part), finish)
     for store in stores:
         store.wait()
 
@@ -320,6 +338,14 @@
         tiled=True,
     )
     recv_other = lax.ppermute(recv, "fsdp", swap)
+    block, part = min(256, hidden), min(256, hidden)
+    blocks = hidden // block
+    anywhere, held = pl.BlockSpec(memory_space=pl.ANY), pl.BlockSpec(memory_space=pltpu.VMEM)
+    dma = pltpu.SemaphoreType.DMA
+
+    def matrix(*shape):
+        return pltpu.VMEM(shape, bf16)
+
     pick = pl.pallas_call(
         functools.partial(place_kernel, plan),
         out_shape=jax.ShapeDtypeStruct((plan.tok_dev, experts * plan.back), bf16),
@@ -327,17 +353,18 @@
         name="placing",
     )(route)
 
-    block, part = min(256, hidden), min(256, hidden)
-    blocks = hidden // block
-    anywhere, held = pl.BlockSpec(memory_space=pl.ANY), pl.BlockSpec(memory_space=pltpu.VMEM)
-    dma = pltpu.SemaphoreType.DMA
-
-    def matrix(*shape):
-        return pltpu.VMEM(shape, bf16)
-
+    firsts = pl.pallas_call(
+        stage_kernel,
+        in_specs=[anywhere] * 3,
+        out_specs=(held,) * 2,
+        out_shape=(jax.ShapeDtypeStruct((width, block), bf16),) * 2,
+        scratch_shapes=[dma((2,))],
+        compiler_params=params(52),
+        name="staging",
+    )(pick, in_own, out_own)
     back = pl.pallas_call(
         functools.partial(token_kernel, plan, part),
-        in_specs=[held] + [anywhere] * 4,
+        in_specs=[held] * 3 + [anywhere] * 4,
         out_specs=held,
         out_shape=jax.ShapeDtypeStruct((experts, plan.back, width), bf16),
         scratch_shapes=[
@@ -355,12 +382,12 @@
         ),
         compiler_params=params(52),
         name="token_grad",
-    )(recv, in_own, out_own, in_other, out_other)
+    )(recv, *firsts, in_own, out_own, in_other, out_other)
     returned = lax.all_to_all(back, "expert", split_axis=0, concat_axis=0, tiled=True)
 
     grad_in, grad_out = pl.pallas_call(
         functools.partial(weight_kernel, plan, part),
-        in_specs=[held, held, anywhere, anywhere],
+        in_specs=[held] * 4 + [anywhere] * 2,
         out_specs=(anywhere, anywhere),
         out_shape=(jax.ShapeDtypeStruct((width, hidden), bf16),) * 2,
         scratch_shapes=[
@@ -382,7 +409,7 @@
         ),
         compiler_params=params(52),
         name="weight_grad",
-    )(recv, recv_other, in_own, out_own)
+    )(recv, recv_other, *firsts, in_own, out_own)
 
     d_tokens, d_gates = pl.pallas_call(
         functools.partial(combine_kernel, plan),

time: 60.2 us -> 60.8 us (level)
  waiting for transfers between devices: 0.5 us -> 2.59 us
  Pallas kernels: 25.5 us -> 24.5 us
    all_to_all x1, waiting for transfers between devices: 0.49 us -> 2.59 us  [moved_rows(): lax.all_to_all(back, 'expert', split_axis=0, concat_axis=0, tiled=True)]
    pallas_call x1, Pallas kernels: 9.51 us -> 8.21 us  [moved_rows(): pl.pallas_call(functools.partial(token_kernel, plan, part), in_specs=[hel...]
    pallas_call x0 -> x1, Pallas kernels: none -> 1.05 us  [moved_rows(): pl.pallas_call(stage_kernel, in_specs=[anywhere] * 3, out_specs=(held,) *...]
    pallas_call x1, Pallas kernels: 11 us -> 10.3 us  [moved_rows(): pl.pallas_call(functools.partial(weight_kernel, plan, part), in_specs=[he...]
  transfers between devices with their start and end apart: 4 -> 4, of which waited for: 1 -> 1; matrix products, arithmetic and copies ran while one was open for 0% -> 0% of each run, Pallas kernels for 41% -> 39%
where the time goes in v1:
time: 60.8 us; the launch traced here: 60.4 us
  blocking collectives  27.3 us (45%)
  Pallas kernels  24.5 us (40%)
  starting transfers between devices  4.39 us (7%)
  waiting for transfers between devices  2.59 us (4%)
  local copies, waits for them, and re-layouts  0.91 us (1%)
  between operations  0.72 us (1%)
    all_to_all x1, blocking collectives, moved_rows(): lax.all_to_all(send.reshape(experts, plan.send, width), 'expert', split_a...  27.3 us
    pallas_call x1, Pallas kernels, moved_rows(): pl.pallas_call(functools.partial(weight_kernel, plan, part), in_specs=[he...  10.3 us
    pallas_call x1, Pallas kernels, moved_rows(): pl.pallas_call(functools.partial(token_kernel, plan, part), in_specs=[hel...  8.21 us
    all_to_all x1, starting transfers between devices, moved_rows(): lax.all_to_all(back, 'expert', split_axis=0, concat_axis=0, tiled=True)  3.74 us
    all_to_all x1, waiting for transfers between devices, moved_rows(): lax.all_to_all(back, 'expert', split_axis=0, concat_axis=0, tiled=True)  2.59 us
    pallas_call x1, Pallas kernels, moved_rows(): pl.pallas_call(functools.partial(dispatch_kernel, plan), out_shape=(jax.S...  2.49 us
    pallas_call x1, Pallas kernels, moved_rows(): pl.pallas_call(functools.partial(place_kernel, plan), out_shape=jax.Shape...  1.43 us
  transfers between devices with their start and end apart: 4, of which 1 were waited for; matrix products, arithmetic and copies ran while one was open for 0% of the time, Pallas kernels for 39%

profile of v1, /device:TPU:0, one launch (start us, length us, event | category | flops | bytes accessed | tf_op | source)
XLA Modules:
  0.0 60.4 jit_solution(11295008614472996109)
XLA Ops:
  0.6 0.6 collective-permute-start
  1.2 0.1 collective-permute-start.1
  1.3 2.5 %dispatch.1 = (bf16[640,512]{1,0:T(8,128)(2,1)}, s32[8,128]{1,0:T(8,128)}) custom-call(s32[2,256]{1,0:T(2,128)} %bitcast.21, bf16[2,256]{1,0:T(2,128)(2,1)} %bitcast.10, bf16[128,512]{1,0:T(8,128)(2,1)} %x_ref.1, bf16[128,512]{1,0:T(8,128)(2,1)} %dy_ref.1), custom_call_target="tpu_custom_call" | custom-call | tf_op jit(solution)/shard_map/dispatch/pallas_call | solution.py:325
  3.8 27.3 %all_to_all.10.recv_ref.own_ref = bf16[16,40,512]{2,1,0:T(8,128)(2,1)S(1)} all-to-all(bf16[16,40,512]{2,1,0:T(8,128)(2,1)} %bitcast.20), channel_id=1, replica_groups=mesh['expert'=16,'fsdp'=2] {'expert'}, dimensions={0} | all-to-all | bytes 1310720 | tf_op jit(solution)/shard_map/all_to_all | solution.py:333
  31.0 0.0 collective-permute-start.2
  31.0 1.4 %placing.1._.pick_ref = bf16[128,384]{1,0:T(8,128)(2,1)} custom-call(s32[8,128]{1,0:T(8,128)} %get-tuple-element.12.route_ref), custom_call_target="tpu_custom_call" | custom-call | tf_op jit(solution)/shard_map/placing/pallas_call | solution.py:349
  32.5 0.0 copy-start
  32.5 0.9 %copy-done = bf16[128,384]{1,0:T(8,128)(2,1)S(1)} copy-done((bf16[128,384]{1,0:T(8,128)(2,1)S(1)}, bf16[128,384]{1,0:T(8,128)(2,1)}, u32[]{:S(2)}) %copy-start) | copy-done | bytes 98328
  33.4 1.0 %staging.1 = (bf16[512,256]{1,0:T(8,128)(2,1)S(1)}, bf16[512,256]{1,0:T(8,128)(2,1)S(1)}) custom-call(bf16[128,384]{1,0:T(8,128)(2,1)S(1)} %copy-done, bf16[512,2048]{1,0:T(8,128)(2,1)} %bitcast.13, bf16[512,2048]{1,0:T(8,128)(2,1)} %bitcast.17), custom_call_target="tpu_custom_call" | custom-call | tf_op jit(solution)/shard_map/staging/pallas_call | solution.py:356
  34.4 0.0 collective-permute-done.in_b
  34.4 0.0 collective-permute-done.1.out_b
  34.4 8.2 %token_grad.1 = bf16[16,24,512]{2,1,0:T(8,128)(2,1)} custom-call(bf16[16,40,512]{2,1,0:T(8,128)(2,1)S(1)} %all_to_all.10.recv_ref.own_ref, bf16[512,256]{1,0:T(8,128)(2,1)S(1)} %get-tuple-element.14.in_first, bf16[512,256]{1,0:T(8,128)(2,1)S(1)} %get-tuple-element.15.out_first, bf16[512,2048]{1,0:T(8,128)(2,1)} %bitcast.14, bf16[512,2048]{1,0:T(8,128)(2,1)} %bitcast.18, ...), custom_call_target="tpu_custom_call" | custom-call | flops 4026531840 | bytes 8388608 | tf_op jit(solution)/shard_map/token_grad/pallas_call | solution.py:365
  42.7 3.7 %all-to-all-start.1 = ((bf16[16,24,512]{2,1,0:T(8,128)(2,1)}), bf16[16,24,512]{2,1,0:T(8,128)(2,1)S(1)}, u32[]{:S(2)}, u32[]{:S(2)}) async-start(bf16[16,24,512]{2,1,0:T(8,128)(2,1)} %token_grad.1), calls=%async_computation.1 | async-start | bytes 786432 | tf_op jit(solution)/shard_map/all_to_all | solution.py:386
  46.4 0.0 copy-start.1
  46.4 0.0 copy-start.2
  46.4 0.0 copy-start.3
  46.4 0.0 collective-permute-done.2.other_ref
  46.4 10.3 %weight_grad.1 = (bf16[512,2048]{1,0:T(8,128)(2,1)}, bf16[512,2048]{1,0:T(8,128)(2,1)}) custom-call(bf16[16,40,512]{2,1,0:T(8,128)(2,1)S(1)} %all_to_all.10.recv_ref.own_ref, bf16[16,40,512]{2,1,0:T(8,128)(2,1)} %collective-permute-done.2.other_ref, bf16[512,256]{1,0:T(8,128)(2,1)S(1)} %get-tuple-element.14.in_first, ...), custom_call_target="tpu_custom_call" | custom-call | flops 5368709120 | bytes 8388608 | tf_op jit(solution)/shard_map/weight_grad/pallas_call | solution.py:388
  56.8 2.6 %all-to-all-done.1 = bf16[16,24,512]{2,1,0:T(8,128)(2,1)S(1)} async-done(((bf16[16,24,512]{2,1,0:T(8,128)(2,1)}), bf16[16,24,512]{2,1,0:T(8,128)(2,1)S(1)}, u32[]{:S(2)}, u32[]{:S(2)}) %all-to-all-start.1) | async-done | bytes 393248 | tf_op jit(solution)/shard_map/all_to_all | solution.py:386
  59.4 0.0 copy-done.1
  59.4 0.0 copy-done.2
  59.4 0.0 copy-done.3
  59.4 1.0 %combine.1 = (bf16[128,512]{1,0:T(8,128)(2,1)}, f32[2,128]{1,0:T(2,128)}) custom-call(s32[8,128]{1,0:T(8,128)S(1)} %copy-done.2, bf16[128,384]{1,0:T(8,128)(2,1)S(1)} %copy-done.1, bf16[2,256]{1,0:T(2,128)(2,1)S(1)} %bitcast.11, bf16[384,512]{1,0:T(8,128)(2,1)S(1)} %bitcast.9), custom_call_target="tpu_custom_call" | custom-call | tf_op jit(solution)/shard_map/combine/pallas_call | solution.py:414
Async XLA Ops:
  0.6 33.8 %collective-permute-start = (bf16[512,2048]{1,0:T(8,128)(2,1)}, bf16[512,2048]{1,0:T(8,128)(2,1)}, u32[]{:S(2)}, u32[]{:S(2)}) collective-permute-start(bf16[512,2048]{1,0:T(8,128)(2,1)} %bitcast.12), channel_id=1, source_target_pairs={{0,1},{1,0},{2,3},{3,2},{4,5},{5,4},{6,7},{7,6},{8,9},{9,8},{10,11... | collective-permute-start | bytes 6291464 | tf_op jit(solution)/shard_map/ppermute | solution.py:320
  1.2 33.2 %collective-permute-start.1 = (bf16[512,2048]{1,0:T(8,128)(2,1)}, bf16[512,2048]{1,0:T(8,128)(2,1)}, u32[]{:S(2)}, u32[]{:S(2)}) collective-permute-start(bf16[512,2048]{1,0:T(8,128)(2,1)} %bitcast.16), channel_id=1, source_target_pairs={{0,1},{1,0},{2,3},{3,2},{4,5},{5,4},{6,7},{7,6},{8,9},{9,8},{10,11... | collective-permute-start | bytes 6291464 | tf_op jit(solution)/shard_map/ppermute | solution.py:321
  31.0 15.4 %collective-permute-start.2 = (bf16[16,40,512]{2,1,0:T(8,128)(2,1)S(1)}, bf16[16,40,512]{2,1,0:T(8,128)(2,1)}, u32[]{:S(2)}, u32[]{:S(2)}) collective-permute-start(bf16[16,40,512]{2,1,0:T(8,128)(2,1)S(1)} %all_to_all.10.recv_ref.own_ref), channel_id=1, source_target_pairs={{0,1},{1,0},{2,3},{3,2},{4,5},{5,4},{6,7},{7,6},{8,9},{9,8},{10,11... | collective-permute-start | bytes 1966088 | tf_op jit(solution)/shard_map/ppermute | solution.py:340
  32.5 0.9 %copy-start = (bf16[128,384]{1,0:T(8,128)(2,1)S(1)}, bf16[128,384]{1,0:T(8,128)(2,1)}, u32[]{:S(2)}) copy-start(bf16[128,384]{1,0:T(8,128)(2,1)} %placing.1._.pick_ref) | copy-start | bytes 294916
  42.7 16.7 %all-to-all-start.1 = ((bf16[16,24,512]{2,1,0:T(8,128)(2,1)}), bf16[16,24,512]{2,1,0:T(8,128)(2,1)S(1)}, u32[]{:S(2)}, u32[]{:S(2)}) async-start(bf16[16,24,512]{2,1,0:T(8,128)(2,1)} %token_grad.1), calls=%async_computation.1 | async-start | bytes 786432 | tf_op jit(solution)/shard_map/all_to_all | solution.py:386
  46.4 13.0 %copy-start.1 = (bf16[128,384]{1,0:T(8,128)(2,1)S(1)}, bf16[128,384]{1,0:T(8,128)(2,1)}, u32[]{:S(2)}) copy-start(bf16[128,384]{1,0:T(8,128)(2,1)} %placing.1._.pick_ref) | copy-start | bytes 294916
  46.4 13.0 %copy-start.2 = (s32[8,128]{1,0:T(8,128)S(1)}, s32[8,128]{1,0:T(8,128)}, u32[]{:S(2)}) copy-start(s32[8,128]{1,0:T(8,128)} %get-tuple-element.12.route_ref) | copy-start | bytes 12292
  46.4 13.0 %copy-start.3 = (bf16[256,2]{0,1:T(2,128)(2,1)S(1)}, bf16[256,2]{0,1:T(2,128)(2,1)}, u32[]{:S(2)}) copy-start(bf16[256,2]{0,1:T(2,128)(2,1)} %param.8) | copy-start | bytes 3076

commit v2 on v1

--- a/solution.py
+++ b/solution.py
@@ -28,6 +28,10 @@
 
 def iota(shape, dim):
     return lax.broadcasted_iota(jnp.int32, shape, dim)
+
+
+def split(value, unit):
+    return value >> (unit.bit_length() - 1), value & (unit - 1)
 
 
 def one_hot(mask):
@@ -97,11 +101,11 @@
         (2 * tails, plan.experts * TILE), 1
     )
     second = jnp.where(place >= tails, 1, 0)
-    slot = place - second * tails
-    pick = one_hot(source == slot // tail * TILE + slot % tail + second * tail)
-    split = jnp.dot(pick, mixed, preferred_element_type=jnp.float32).astype(jnp.bfloat16)
-    x_all[pl.ds(at + plan.heads, tails), :] = split[:tails]
-    dy_all[pl.ds(at + plan.heads, tails), :] = split[tails:]
+    block, rank = split(place - second * tails, tail)
+    pick = one_hot(source == block * TILE + rank + second * tail)
+    rows = jnp.dot(pick, mixed, preferred_element_type=jnp.float32).astype(jnp.bfloat16)
+    x_all[pl.ds(at + plan.heads, tails), :] = rows[:tails]
+    dy_all[pl.ds(at + plan.heads, tails), :] = rows[tails:]
 
 
 def stage_kernel(_, in_hbm, out_hbm, in_first, out_first, sems):
@@ -165,7 +169,7 @@
 
 
 def token_kernel(
-    plan, part, recv_ref, in_first, out_first, in_a, out_a, in_b, out_b, back_ref, x_all, dy_all, total, in_buf, out_buf, sems
+    plan, part, recv_ref, in_first, out_first, in_a, out_a, in_b, out_b, back_hbm, x_all, dy_all, total, in_buf, out_buf, heads, rests, sems, store_sems
 ):
     buffers, firsts = (in_buf, out_buf), (in_first, out_first)
     copies = column_copies(((in_a, out_a), (in_b, out_b)), buffers, sems)
@@ -195,29 +199,41 @@
 
     main, tail, width = plan.main, plan.tail, plan.width
     tails = plan.experts * tail
-    rows = total[...].astype(jnp.bfloat16)
-    back_ref[:, :main, :] = rows[: plan.heads].reshape(plan.experts, main, width)
+    stores = [
+        pltpu.make_async_copy(heads, back_hbm.at[:, :main, :], store_sems.at[0]),
+        pltpu.make_async_copy(rests, back_hbm.at[:, main:, :], store_sems.at[1]),
+    ]
+    heads[...] = (
+        total[: plan.heads, :].astype(jnp.bfloat16).reshape(plan.experts, main, width)
+    )
+    stores[0].start()
     gate = jnp.sum(gate_lanes[0], axis=1, keepdims=True)
-    slot = iota((plan.slots, LANES), 0)
-    over = slot - plan.heads
-    rank = jnp.where(over >= 0, main + over % tail, slot % main)
+
+    def place_of(slot):
+        source, rank = split(slot, main)
+        block, over = split(slot - plan.heads, tail)
+        late = slot >= plan.heads
+        return jnp.where(late, block, source), jnp.where(late, main + over, rank)
+
+    _, rank = place_of(iota((plan.slots, LANES), 0))
     gate_rows = jnp.where(iota((plan.slots, LANES), 1) == rank, gate, 0.0).astype(jnp.bfloat16)
-    place, slot = iota((plan.experts * TILE, plan.slots), 0), iota(
-        (plan.experts * TILE, plan.slots), 1
-    )
-    over = slot - plan.heads
-    source = jnp.where(over >= 0, over // tail, slot // main)
+    place = iota((plan.experts * TILE, plan.slots), 0)
+    source, _ = place_of(iota((plan.experts * TILE, plan.slots), 1))
     gates = jnp.dot(
         one_hot(place == source * TILE + tail), gate_rows, preferred_element_type=jnp.float32
     )
-    place, slot = iota((plan.experts * TILE, tails), 0), iota((plan.experts * TILE, tails), 1)
+    place = iota((plan.experts * TILE, tails), 0)
+    block, over = split(iota((plan.experts * TILE, tails), 1), tail)
     rest = jnp.dot(
-        one_hot(place == slot // tail * TILE + slot % tail),
-        rows[plan.heads :],
+        one_hot(place == block * TILE + over),
+        total[plan.heads :, :].astype(jnp.bfloat16),
         preferred_element_type=jnp.float32,
     )
     rest = jnp.concatenate([rest[:, :LANES] + gates, rest[:, LANES:]], axis=1)
-    back_ref[:, main:, :] = rest.astype(jnp.bfloat16).reshape(plan.experts, TILE, width)
+    rests[...] = rest.astype(jnp.bfloat16).reshape(plan.experts, TILE, width)
+    stores[1].start()
+    for store in stores:
+        store.wait()
 
 
 def weight_kernel(
@@ -365,7 +381,7 @@
     back = pl.pallas_call(
         functools.partial(token_kernel, plan, part),
         in_specs=[held] * 3 + [anywhere] * 4,
-        out_specs=held,
+        out_specs=anywhere,
         out_shape=jax.ShapeDtypeStruct((experts, plan.back, width), bf16),
         scratch_shapes=[
             matrix(slots, width),
@@ -373,7 +389,10 @@
             pltpu.VMEM((slots, width), f32),
             matrix(2 * blocks, width, block),
             matrix(2 * blocks, width, block),
+            matrix(experts, plan.main, width),
+            matrix(experts, TILE, width),
             dma((2, 2 * blocks)),
+            dma((2,)),
         ],
         cost_estimate=pl.CostEstimate(
             flops=12 * slots * width * hidden,

time: 60.8 us -> 60.8 us (level)
  no operation moved by 1% of the time
where the time goes in v2:
time: 60.8 us; the launch traced here: 60.3 us
  blocking collectives  27.3 us (45%)
  Pallas kernels  24.5 us (40%)
  starting transfers between devices  4.39 us (7%)
  waiting for transfers between devices  2.59 us (4%)
  local copies, waits for them, and re-layouts  0.91 us (1%)
  between operations  0.72 us (1%)
    all_to_all x1, blocking collectives, moved_rows(): lax.all_to_all(send.reshape(experts, plan.send, width), 'expert', split_a...  27.3 us
    pallas_call x1, Pallas kernels, moved_rows(): pl.pallas_call(functools.partial(weight_kernel, plan, part), in_specs=[he...  10.3 us
    pallas_call x1, Pallas kernels, moved_rows(): pl.pallas_call(functools.partial(token_kernel, plan, part), in_specs=[hel...  8.14 us
    all_to_all x1, starting transfers between devices, moved_rows(): lax.all_to_all(back, 'expert', split_axis=0, concat_axis=0, tiled=True)  3.74 us
    all_to_all x1, waiting for transfers between devices, moved_rows(): lax.all_to_all(back, 'expert', split_axis=0, concat_axis=0, tiled=True)  2.59 us
    pallas_call x1, Pallas kernels, moved_rows(): pl.pallas_call(functools.partial(dispatch_kernel, plan), out_shape=(jax.S...  2.49 us
    pallas_call x1, Pallas kernels, moved_rows(): pl.pallas_call(functools.partial(place_kernel, plan), out_shape=jax.Shape...  1.43 us
  transfers between devices with their start and end apart: 4, of which 1 were waited for; matrix products, arithmetic and copies ran while one was open for 0% of the time, Pallas kernels for 39%

profile of v2, /device:TPU:0, one launch (start us, length us, event | category | flops | bytes accessed | tf_op | source)
XLA Modules:
  0.0 60.3 jit_solution(10477282124036621024)
XLA Ops:
  0.6 0.6 collective-permute-start
  1.2 0.1 collective-permute-start.1
  1.3 2.5 %dispatch.1 = (bf16[640,512]{1,0:T(8,128)(2,1)}, s32[8,128]{1,0:T(8,128)}) custom-call(s32[2,256]{1,0:T(2,128)} %bitcast.21, bf16[2,256]{1,0:T(2,128)(2,1)} %bitcast.10, bf16[128,512]{1,0:T(8,128)(2,1)} %x_ref.1, bf16[128,512]{1,0:T(8,128)(2,1)} %dy_ref.1), custom_call_target="tpu_custom_call" | custom-call | tf_op jit(solution)/shard_map/dispatch/pallas_call | solution.py:341
  3.8 27.3 %all_to_all.10.recv_ref.own_ref = bf16[16,40,512]{2,1,0:T(8,128)(2,1)S(1)} all-to-all(bf16[16,40,512]{2,1,0:T(8,128)(2,1)} %bitcast.20), channel_id=1, replica_groups=mesh['expert'=16,'fsdp'=2] {'expert'}, dimensions={0} | all-to-all | bytes 1310720 | tf_op jit(solution)/shard_map/all_to_all | solution.py:349
  31.0 0.0 collective-permute-start.2
  31.0 1.4 %placing.1._.pick_ref = bf16[128,384]{1,0:T(8,128)(2,1)} custom-call(s32[8,128]{1,0:T(8,128)} %get-tuple-element.12.route_ref), custom_call_target="tpu_custom_call" | custom-call | tf_op jit(solution)/shard_map/placing/pallas_call | solution.py:365
  32.5 0.0 copy-start
  32.5 0.9 %copy-done = bf16[128,384]{1,0:T(8,128)(2,1)S(1)} copy-done((bf16[128,384]{1,0:T(8,128)(2,1)S(1)}, bf16[128,384]{1,0:T(8,128)(2,1)}, u32[]{:S(2)}) %copy-start) | copy-done | bytes 98328
  33.4 1.0 %staging.1 = (bf16[512,256]{1,0:T(8,128)(2,1)S(1)}, bf16[512,256]{1,0:T(8,128)(2,1)S(1)}) custom-call(bf16[128,384]{1,0:T(8,128)(2,1)S(1)} %copy-done, bf16[512,2048]{1,0:T(8,128)(2,1)} %bitcast.13, bf16[512,2048]{1,0:T(8,128)(2,1)} %bitcast.17), custom_call_target="tpu_custom_call" | custom-call | tf_op jit(solution)/shard_map/staging/pallas_call | solution.py:372
  34.4 0.0 collective-permute-done.in_b
  34.4 0.0 collective-permute-done.1.out_b
  34.4 8.1 %token_grad.1 = bf16[16,24,512]{2,1,0:T(8,128)(2,1)} custom-call(bf16[16,40,512]{2,1,0:T(8,128)(2,1)S(1)} %all_to_all.10.recv_ref.own_ref, bf16[512,256]{1,0:T(8,128)(2,1)S(1)} %get-tuple-element.14.in_first, bf16[512,256]{1,0:T(8,128)(2,1)S(1)} %get-tuple-element.15.out_first, bf16[512,2048]{1,0:T(8,128)(2,1)} %bitcast.14, bf16[512,2048]{1,0:T(8,128)(2,1)} %bitcast.18, ...), custom_call_target="tpu_custom_call" | custom-call | flops 4026531840 | bytes 8388608 | tf_op jit(solution)/shard_map/token_grad/pallas_call | solution.py:381
  42.6 3.7 %all-to-all-start.1 = ((bf16[16,24,512]{2,1,0:T(8,128)(2,1)}), bf16[16,24,512]{2,1,0:T(8,128)(2,1)S(1)}, u32[]{:S(2)}, u32[]{:S(2)}) async-start(bf16[16,24,512]{2,1,0:T(8,128)(2,1)} %token_grad.1), calls=%async_computation.1 | async-start | bytes 786432 | tf_op jit(solution)/shard_map/all_to_all | solution.py:405
  46.3 0.0 copy-start.1
  46.3 0.0 copy-start.2
  46.4 0.0 copy-start.3
  46.4 0.0 collective-permute-done.2.other_ref
  46.4 10.3 %weight_grad.1 = (bf16[512,2048]{1,0:T(8,128)(2,1)}, bf16[512,2048]{1,0:T(8,128)(2,1)}) custom-call(bf16[16,40,512]{2,1,0:T(8,128)(2,1)S(1)} %all_to_all.10.recv_ref.own_ref, bf16[16,40,512]{2,1,0:T(8,128)(2,1)} %collective-permute-done.2.other_ref, bf16[512,256]{1,0:T(8,128)(2,1)S(1)} %get-tuple-element.14.in_first, ...), custom_call_target="tpu_custom_call" | custom-call | flops 5368709120 | bytes 8388608 | tf_op jit(solution)/shard_map/weight_grad/pallas_call | solution.py:407
  56.7 2.6 %all-to-all-done.1 = bf16[16,24,512]{2,1,0:T(8,128)(2,1)S(1)} async-done(((bf16[16,24,512]{2,1,0:T(8,128)(2,1)}), bf16[16,24,512]{2,1,0:T(8,128)(2,1)S(1)}, u32[]{:S(2)}, u32[]{:S(2)}) %all-to-all-start.1) | async-done | bytes 393248 | tf_op jit(solution)/shard_map/all_to_all | solution.py:405
  59.3 0.0 copy-done.1
  59.3 0.0 copy-done.2
  59.3 0.0 copy-done.3
  59.3 1.0 %combine.1 = (bf16[128,512]{1,0:T(8,128)(2,1)}, f32[2,128]{1,0:T(2,128)}) custom-call(s32[8,128]{1,0:T(8,128)S(1)} %copy-done.2, bf16[128,384]{1,0:T(8,128)(2,1)S(1)} %copy-done.1, bf16[2,256]{1,0:T(2,128)(2,1)S(1)} %bitcast.11, bf16[384,512]{1,0:T(8,128)(2,1)S(1)} %bitcast.9), custom_call_target="tpu_custom_call" | custom-call | tf_op jit(solution)/shard_map/combine/pallas_call | solution.py:433
Async XLA Ops:
  0.6 33.8 %collective-permute-start = (bf16[512,2048]{1,0:T(8,128)(2,1)}, bf16[512,2048]{1,0:T(8,128)(2,1)}, u32[]{:S(2)}, u32[]{:S(2)}) collective-permute-start(bf16[512,2048]{1,0:T(8,128)(2,1)} %bitcast.12), channel_id=1, source_target_pairs={{0,1},{1,0},{2,3},{3,2},{4,5},{5,4},{6,7},{7,6},{8,9},{9,8},{10,11... | collective-permute-start | bytes 6291464 | tf_op jit(solution)/shard_map/ppermute | solution.py:336
  1.2 33.2 %collective-permute-start.1 = (bf16[512,2048]{1,0:T(8,128)(2,1)}, bf16[512,2048]{1,0:T(8,128)(2,1)}, u32[]{:S(2)}, u32[]{:S(2)}) collective-permute-start(bf16[512,2048]{1,0:T(8,128)(2,1)} %bitcast.16), channel_id=1, source_target_pairs={{0,1},{1,0},{2,3},{3,2},{4,5},{5,4},{6,7},{7,6},{8,9},{9,8},{10,11... | collective-permute-start | bytes 6291464 | tf_op jit(solution)/shard_map/ppermute | solution.py:337
  31.0 15.3 %collective-permute-start.2 = (bf16[16,40,512]{2,1,0:T(8,128)(2,1)S(1)}, bf16[16,40,512]{2,1,0:T(8,128)(2,1)}, u32[]{:S(2)}, u32[]{:S(2)}) collective-permute-start(bf16[16,40,512]{2,1,0:T(8,128)(2,1)S(1)} %all_to_all.10.recv_ref.own_ref), channel_id=1, source_target_pairs={{0,1},{1,0},{2,3},{3,2},{4,5},{5,4},{6,7},{7,6},{8,9},{9,8},{10,11... | collective-permute-start | bytes 1966088 | tf_op jit(solution)/shard_map/ppermute | solution.py:356
  32.5 0.9 %copy-start = (bf16[128,384]{1,0:T(8,128)(2,1)S(1)}, bf16[128,384]{1,0:T(8,128)(2,1)}, u32[]{:S(2)}) copy-start(bf16[128,384]{1,0:T(8,128)(2,1)} %placing.1._.pick_ref) | copy-start | bytes 294916
  42.6 16.7 %all-to-all-start.1 = ((bf16[16,24,512]{2,1,0:T(8,128)(2,1)}), bf16[16,24,512]{2,1,0:T(8,128)(2,1)S(1)}, u32[]{:S(2)}, u32[]{:S(2)}) async-start(bf16[16,24,512]{2,1,0:T(8,128)(2,1)} %token_grad.1), calls=%async_computation.1 | async-start | bytes 786432 | tf_op jit(solution)/shard_map/all_to_all | solution.py:405
  46.3 13.0 %copy-start.1 = (bf16[128,384]{1,0:T(8,128)(2,1)S(1)}, bf16[128,384]{1,0:T(8,128)(2,1)}, u32[]{:S(2)}) copy-start(bf16[128,384]{1,0:T(8,128)(2,1)} %placing.1._.pick_ref) | copy-start | bytes 294916
  46.3 13.0 %copy-start.2 = (s32[8,128]{1,0:T(8,128)S(1)}, s32[8,128]{1,0:T(8,128)}, u32[]{:S(2)}) copy-start(s32[8,128]{1,0:T(8,128)} %get-tuple-element.12.route_ref) | copy-start | bytes 12292
  46.4 13.0 %copy-start.3 = (bf16[256,2]{0,1:T(2,128)(2,1)S(1)}, bf16[256,2]{0,1:T(2,128)(2,1)}, u32[]{:S(2)}) copy-start(bf16[256,2]{0,1:T(2,128)(2,1)} %param.8) | copy-start | bytes 3076

commit v3 on v2

--- a/solution.py
+++ b/solution.py
@@ -16,6 +16,7 @@
 TILE = 8
 PACK = 16
 MIB = 1 << 20
+GROUP = 3
 
 
 def gelu_parts(pre_act):
@@ -150,14 +151,15 @@
     return first[:, at : at + part] if chunk == 0 else buffer[chunk, :, at : at + part]
 
 
-def first_acts(x_all, dy_all, firsts, buffers, copies, part):
+def first_acts(x_all, dy_all, firsts, buffers, copies, part, group=1):
     block = buffers[0].shape[2]
 
     def ahead(n):
         chunk, at = divmod(n * part, block)
-        if at == 0 and chunk > 0:
-            for copy in copies[chunk]:
-                copy.wait()
+        if at == 0 and chunk % group == 1 % group:
+            for pair in copies[max(chunk, 1) : chunk + group]:
+                for copy in pair:
+                    copy.wait()
         return tuple(
             jnp.dot(
                 rows[...], part_of(first, mat, n, part), preferred_element_type=jnp.float32
@@ -195,7 +197,7 @@
             piece = product[:, lane : lane + LANES]
             gate_lanes[:] = [gate_lanes[0] + piece] if gate_lanes else [piece]
 
-    staged(len(copies) * block // part, first_acts(x_all, dy_all, firsts, buffers, copies, part), finish)
+    staged(len(copies) * block // part, first_acts(x_all, dy_all, firsts, buffers, copies, part, GROUP), finish)
 
     main, tail, width = plan.main, plan.tail, plan.width
     tails = plan.experts * tail

time: 60.8 us -> 60.6 us (level)
  no operation moved by 1% of the time
where the time goes in v3:
time: 60.6 us; the launch traced here: 60.2 us
  blocking collectives  27.3 us (45%)
  Pallas kernels  24.3 us (40%)
  starting transfers between devices  4.39 us (7%)
  waiting for transfers between devices  2.59 us (4%)
  local copies, waits for them, and re-layouts  0.91 us (2%)
  between operations  0.72 us (1%)
    all_to_all x1, blocking collectives, moved_rows(): lax.all_to_all(send.reshape(experts, plan.send, width), 'expert', split_a...  27.3 us
    pallas_call x1, Pallas kernels, moved_rows(): pl.pallas_call(functools.partial(weight_kernel, plan, part), in_specs=[he...  10.3 us
    pallas_call x1, Pallas kernels, moved_rows(): pl.pallas_call(functools.partial(token_kernel, plan, part), in_specs=[hel...  8 us
    all_to_all x1, starting transfers between devices, moved_rows(): lax.all_to_all(back, 'expert', split_axis=0, concat_axis=0, tiled=True)  3.74 us
    all_to_all x1, waiting for transfers between devices, moved_rows(): lax.all_to_all(back, 'expert', split_axis=0, concat_axis=0, tiled=True)  2.58 us
    pallas_call x1, Pallas kernels, moved_rows(): pl.pallas_call(functools.partial(dispatch_kernel, plan), out_shape=(jax.S...  2.49 us
    pallas_call x1, Pallas kernels, moved_rows(): pl.pallas_call(functools.partial(place_kernel, plan), out_shape=jax.Shape...  1.43 us
  transfers between devices with their start and end apart: 4, of which 1 were waited for; matrix products, arithmetic and copies ran while one was open for 0% of the time, Pallas kernels for 39%

profile of v3, /device:TPU:0, one launch (start us, length us, event | category | flops | bytes accessed | tf_op | source)
XLA Modules:
  0.0 60.2 jit_solution(6122587488634466945)
XLA Ops:
  0.6 0.6 collective-permute-start
  1.2 0.1 collective-permute-start.1
  1.3 2.5 %dispatch.1 = (bf16[640,512]{1,0:T(8,128)(2,1)}, s32[8,128]{1,0:T(8,128)}) custom-call(s32[2,256]{1,0:T(2,128)} %bitcast.21, bf16[2,256]{1,0:T(2,128)(2,1)} %bitcast.10, bf16[128,512]{1,0:T(8,128)(2,1)} %x_ref.1, bf16[128,512]{1,0:T(8,128)(2,1)} %dy_ref.1), custom_call_target="tpu_custom_call" | custom-call | tf_op jit(solution)/shard_map/dispatch/pallas_call | solution.py:343
  3.8 27.3 %all_to_all.10.recv_ref.own_ref = bf16[16,40,512]{2,1,0:T(8,128)(2,1)S(1)} all-to-all(bf16[16,40,512]{2,1,0:T(8,128)(2,1)} %bitcast.20), channel_id=1, replica_groups=mesh['expert'=16,'fsdp'=2] {'expert'}, dimensions={0} | all-to-all | bytes 1310720 | tf_op jit(solution)/shard_map/all_to_all | solution.py:351
  31.0 0.0 collective-permute-start.2
  31.0 1.4 %placing.1._.pick_ref = bf16[128,384]{1,0:T(8,128)(2,1)} custom-call(s32[8,128]{1,0:T(8,128)} %get-tuple-element.12.route_ref), custom_call_target="tpu_custom_call" | custom-call | tf_op jit(solution)/shard_map/placing/pallas_call | solution.py:367
  32.5 0.0 copy-start
  32.5 0.9 %copy-done = bf16[128,384]{1,0:T(8,128)(2,1)S(1)} copy-done((bf16[128,384]{1,0:T(8,128)(2,1)S(1)}, bf16[128,384]{1,0:T(8,128)(2,1)}, u32[]{:S(2)}) %copy-start) | copy-done | bytes 98328
  33.4 1.0 %staging.1 = (bf16[512,256]{1,0:T(8,128)(2,1)S(1)}, bf16[512,256]{1,0:T(8,128)(2,1)S(1)}) custom-call(bf16[128,384]{1,0:T(8,128)(2,1)S(1)} %copy-done, bf16[512,2048]{1,0:T(8,128)(2,1)} %bitcast.13, bf16[512,2048]{1,0:T(8,128)(2,1)} %bitcast.17), custom_call_target="tpu_custom_call" | custom-call | tf_op jit(solution)/shard_map/staging/pallas_call | solution.py:374
  34.4 0.0 collective-permute-done.in_b
  34.4 0.0 collective-permute-done.1.out_b
  34.4 8.0 %token_grad.1 = bf16[16,24,512]{2,1,0:T(8,128)(2,1)} custom-call(bf16[16,40,512]{2,1,0:T(8,128)(2,1)S(1)} %all_to_all.10.recv_ref.own_ref, bf16[512,256]{1,0:T(8,128)(2,1)S(1)} %get-tuple-element.14.in_first, bf16[512,256]{1,0:T(8,128)(2,1)S(1)} %get-tuple-element.15.out_first, bf16[512,2048]{1,0:T(8,128)(2,1)} %bitcast.14, bf16[512,2048]{1,0:T(8,128)(2,1)} %bitcast.18, ...), custom_call_target="tpu_custom_call" | custom-call | flops 4026531840 | bytes 8388608 | tf_op jit(solution)/shard_map/token_grad/pallas_call | solution.py:383
  42.4 3.7 %all-to-all-start.1 = ((bf16[16,24,512]{2,1,0:T(8,128)(2,1)}), bf16[16,24,512]{2,1,0:T(8,128)(2,1)S(1)}, u32[]{:S(2)}, u32[]{:S(2)}) async-start(bf16[16,24,512]{2,1,0:T(8,128)(2,1)} %token_grad.1), calls=%async_computation.1 | async-start | bytes 786432 | tf_op jit(solution)/shard_map/all_to_all | solution.py:407
  46.2 0.0 copy-start.1
  46.2 0.0 copy-start.2
  46.2 0.0 copy-start.3
  46.2 0.0 collective-permute-done.2.other_ref
  46.2 10.3 %weight_grad.1 = (bf16[512,2048]{1,0:T(8,128)(2,1)}, bf16[512,2048]{1,0:T(8,128)(2,1)}) custom-call(bf16[16,40,512]{2,1,0:T(8,128)(2,1)S(1)} %all_to_all.10.recv_ref.own_ref, bf16[16,40,512]{2,1,0:T(8,128)(2,1)} %collective-permute-done.2.other_ref, bf16[512,256]{1,0:T(8,128)(2,1)S(1)} %get-tuple-element.14.in_first, ...), custom_call_target="tpu_custom_call" | custom-call | flops 5368709120 | bytes 8388608 | tf_op jit(solution)/shard_map/weight_grad/pallas_call | solution.py:409
  56.6 2.6 %all-to-all-done.1 = bf16[16,24,512]{2,1,0:T(8,128)(2,1)S(1)} async-done(((bf16[16,24,512]{2,1,0:T(8,128)(2,1)}), bf16[16,24,512]{2,1,0:T(8,128)(2,1)S(1)}, u32[]{:S(2)}, u32[]{:S(2)}) %all-to-all-start.1) | async-done | bytes 393248 | tf_op jit(solution)/shard_map/all_to_all | solution.py:407
  59.2 0.0 copy-done.1
  59.2 0.0 copy-done.2
  59.2 0.0 copy-done.3
  59.2 1.0 %combine.1 = (bf16[128,512]{1,0:T(8,128)(2,1)}, f32[2,128]{1,0:T(2,128)}) custom-call(s32[8,128]{1,0:T(8,128)S(1)} %copy-done.2, bf16[128,384]{1,0:T(8,128)(2,1)S(1)} %copy-done.1, bf16[2,256]{1,0:T(2,128)(2,1)S(1)} %bitcast.11, bf16[384,512]{1,0:T(8,128)(2,1)S(1)} %bitcast.9), custom_call_target="tpu_custom_call" | custom-call | tf_op jit(solution)/shard_map/combine/pallas_call | solution.py:435
Async XLA Ops:
  0.6 33.8 %collective-permute-start = (bf16[512,2048]{1,0:T(8,128)(2,1)}, bf16[512,2048]{1,0:T(8,128)(2,1)}, u32[]{:S(2)}, u32[]{:S(2)}) collective-permute-start(bf16[512,2048]{1,0:T(8,128)(2,1)} %bitcast.12), channel_id=1, source_target_pairs={{0,1},{1,0},{2,3},{3,2},{4,5},{5,4},{6,7},{7,6},{8,9},{9,8},{10,11... | collective-permute-start | bytes 6291464 | tf_op jit(solution)/shard_map/ppermute | solution.py:338
  1.2 33.2 %collective-permute-start.1 = (bf16[512,2048]{1,0:T(8,128)(2,1)}, bf16[512,2048]{1,0:T(8,128)(2,1)}, u32[]{:S(2)}, u32[]{:S(2)}) collective-permute-start(bf16[512,2048]{1,0:T(8,128)(2,1)} %bitcast.16), channel_id=1, source_target_pairs={{0,1},{1,0},{2,3},{3,2},{4,5},{5,4},{6,7},{7,6},{8,9},{9,8},{10,11... | collective-permute-start | bytes 6291464 | tf_op jit(solution)/shard_map/ppermute | solution.py:339
  31.0 15.2 %collective-permute-start.2 = (bf16[16,40,512]{2,1,0:T(8,128)(2,1)S(1)}, bf16[16,40,512]{2,1,0:T(8,128)(2,1)}, u32[]{:S(2)}, u32[]{:S(2)}) collective-permute-start(bf16[16,40,512]{2,1,0:T(8,128)(2,1)S(1)} %all_to_all.10.recv_ref.own_ref), channel_id=1, source_target_pairs={{0,1},{1,0},{2,3},{3,2},{4,5},{5,4},{6,7},{7,6},{8,9},{9,8},{10,11... | collective-permute-start | bytes 1966088 | tf_op jit(solution)/shard_map/ppermute | solution.py:358
  32.5 0.9 %copy-start = (bf16[128,384]{1,0:T(8,128)(2,1)S(1)}, bf16[128,384]{1,0:T(8,128)(2,1)}, u32[]{:S(2)}) copy-start(bf16[128,384]{1,0:T(8,128)(2,1)} %placing.1._.pick_ref) | copy-start | bytes 294916
  42.4 16.7 %all-to-all-start.1 = ((bf16[16,24,512]{2,1,0:T(8,128)(2,1)}), bf16[16,24,512]{2,1,0:T(8,128)(2,1)S(1)}, u32[]{:S(2)}, u32[]{:S(2)}) async-start(bf16[16,24,512]{2,1,0:T(8,128)(2,1)} %token_grad.1), calls=%async_computation.1 | async-start | bytes 786432 | tf_op jit(solution)/shard_map/all_to_all | solution.py:407
  46.2 13.0 %copy-start.1 = (bf16[128,384]{1,0:T(8,128)(2,1)S(1)}, bf16[128,384]{1,0:T(8,128)(2,1)}, u32[]{:S(2)}) copy-start(bf16[128,384]{1,0:T(8,128)(2,1)} %placing.1._.pick_ref) | copy-start | bytes 294916
  46.2 13.0 %copy-start.2 = (s32[8,128]{1,0:T(8,128)S(1)}, s32[8,128]{1,0:T(8,128)}, u32[]{:S(2)}) copy-start(s32[8,128]{1,0:T(8,128)} %get-tuple-element.12.route_ref) | copy-start | bytes 12292
  46.2 13.0 %copy-start.3 = (bf16[256,2]{0,1:T(2,128)(2,1)S(1)}, bf16[256,2]{0,1:T(2,128)(2,1)}, u32[]{:S(2)}) copy-start(bf16[256,2]{0,1:T(2,128)(2,1)} %param.8) | copy-start | bytes 3076
